TPU v7x, 32 devices: a whole 2x2x4 slice. The times are simulated.
32 devices in a mesh: tp: 2 (over x), ctx: 4 (over y, core), rep: 4 (over z).
Axes of the slice: x: 2, y: 2, z: 4, core: 2. Of those that a mesh axis runs over, the one named last changes fastest.
Arguments:
- tokens: bfloat16 [4, 4, 336, 2048], P('rep', 'ctx', 'tp'), may hold values from -6 to 6
- cotangent: bfloat16 [4, 4, 336, 2048], P('rep', 'ctx', 'tp'), may hold values from -6 to 6
- positions: int32 [4, 1344], P('rep', 'ctx'), may hold values from 0 to 647, as said below
- seg_start: int32 [4, 13], P('rep'), may hold values from 0 to 1272, as said below
- seg_parent: int32 [4, 13], P('rep'), may hold values from 0 to 4, as said below
- ln_gain: bfloat16 [2048], replicated, may hold values from 0.5 to 1.5
- ln_bias: bfloat16 [2048], replicated, may hold values from -1.25 to 1.25
- w_qkv: bfloat16 [2048, 3, 2048], P(None, None, 'tp'), may hold values from -0.125 to 0.125
- b_qkv: bfloat16 [3, 2048], P(None, 'tp'), may hold values from -0.3125 to 0.3125
- w_dense: bfloat16 [2048, 2048], P('tp'), may hold values from -2 to 2
- b_dense: bfloat16 [2048], replicated, may hold values from -1.25 to 1.25
- w_fc1: bfloat16 [2048, 8192], P(None, 'tp'), may hold values from -0.125 to 0.125
- b_fc1: bfloat16 [8192], P('tp'), may hold values from -3 to 3
- w_fc2: bfloat16 [8192, 2048], P('tp'), may hold values from -0.0625 to 0.0625
- b_fc2: bfloat16 [2048], replicated, may hold values from -1.25 to 1.25
Outputs:
- block_out: bfloat16 [4, 4, 336, 2048], P('rep', 'ctx', 'tp')
- d_tokens: float32 [4, 4, 336, 2048], P('rep', 'ctx', 'tp')
- g_ln_gain: float32 [2048], P(('tp', 'ctx', 'rep'))
- g_ln_bias: float32 [2048], P(('tp', 'ctx', 'rep'))
- g_qkv: float32 [2048, 3, 2048], P(('ctx', 'rep'), None, 'tp')
- g_qkv_bias: float32 [3, 2048], P(None, ('tp', 'ctx', 'rep'))
- g_dense: float32 [2048, 2048], P(('tp', 'ctx', 'rep'))
- g_dense_bias: float32 [2048], P(('tp', 'ctx', 'rep'))
- g_fc1: float32 [2048, 8192], P(('ctx', 'rep'), 'tp')
- g_fc1_bias: float32 [8192], P(('tp', 'ctx', 'rep'))
- g_fc2: float32 [8192, 2048], P(('tp', 'ctx', 'rep'))
- g_fc2_bias: float32 [2048], P(('tp', 'ctx', 'rep'))
Inputs may be any that keep to these rules, and one draw needn't show every extreme that they name: Each tree is packed as its trunk (segment 0), then its four branches (segments 1 to 4), then its eight leaves (segments 5 to 12); seg_start rises and its first entry is 0; every segment holds at least one token; seg_start[s + 1] - seg_start[s] and 1344 - seg_start[12] are the lengths. `seg_parent`: the trunk and the branches name 0; each leaf names a branch, and every branch has exactly two leaves. `positions`: A token's offset in its segment plus the lengths of its ancestor segments.
All inputs are finite; a program needn't handle non-finite values.
Results may differ from a plain program's by a relative error of at most 0.014.
Values may be sent and summed in bfloat16 or wider, within the bound.
A program may use at most 320 MiB of HBM per device.

v0:
```python
import math

import jax
import jax.numpy as jnp
from jax import lax
from jax.sharding import PartitionSpec as P

HEAD = 64
ROT = 32


norm_eps = 1e-05
masked_low = -1e30
gelu_root = 0.7978845608028654
gelu_cube = 0.044715


def gelu_tanh(values):
    return (
        0.5 * values * (1.0 + jnp.tanh(gelu_root * (values + gelu_cube * values * values * values)))
    )


def gelu_slope(values):
    tangent = jnp.tanh(gelu_root * (values + gelu_cube * values * values * values))
    return 0.5 * (1.0 + tangent) + 0.5 * values * (1.0 - tangent * tangent) * gelu_root * (
        1.0 + 3.0 * gelu_cube * values * values
    )


def segment_of(token_index, starts):
    return jnp.sum((starts[None, :] <= token_index[:, None]).astype(jnp.int32), axis=1) - 1


def parent_of(segment, parents):
    hits = segment[:, None] == jnp.arange(parents.shape[0], dtype=jnp.int32)[None, :]
    return jnp.sum(jnp.where(hits, parents[None, :], 0), axis=1)


def rotary_tables(token_pos):
    freq_index = jnp.arange(ROT // 2, dtype=jnp.float32)
    inverse = jnp.power(10000.0, -2.0 * freq_index / ROT)
    angles = token_pos.astype(jnp.float32)[:, None] * inverse[None, :]
    return (jnp.cos(angles), jnp.sin(angles))


def rotate(values, cosine, sine):
    half_rot = ROT // 2
    first = values[..., :half_rot]
    second = values[..., half_rot:ROT]
    cos_wide = cosine[:, None, :]
    sin_wide = sine[:, None, :]
    return jnp.concatenate(
        [
            first * cos_wide - second * sin_wide,
            second * cos_wide + first * sin_wide,
            values[..., ROT:],
        ],
        axis=-1,
    )


def rotate_back(grads_in, cosine, sine):
    half_rot = ROT // 2
    first = grads_in[..., :half_rot]
    second = grads_in[..., half_rot:ROT]
    cos_wide = cosine[:, None, :]
    sin_wide = sine[:, None, :]
    return jnp.concatenate(
        [
            first * cos_wide + second * sin_wide,
            second * cos_wide - first * sin_wide,
            grads_in[..., ROT:],
        ],
        axis=-1,
    )


def query_details(query_index, starts, parents):
    own_seg = segment_of(query_index, starts)
    up_one = parent_of(own_seg, parents)
    up_two = parent_of(up_one, parents)
    return (query_index, own_seg, up_one, up_two)


def visible_pairs(query_info, key_index, starts):
    query_index, own_seg, up_one, up_two = query_info
    key_seg = segment_of(key_index, starts)
    related = (
        (key_seg[None, :] == own_seg[:, None])
        | (key_seg[None, :] == up_one[:, None])
        | (key_seg[None, :] == up_two[:, None])
    )
    return related & (key_index[None, :] <= query_index[:, None])


def value_grad(weights, grad_high, grad_rest):
    weights_low = weights.astype(jnp.bfloat16)
    return jnp.einsum(
        "qhk,qhd->khd", weights_low, grad_high, preferred_element_type=jnp.float32
    ) + jnp.einsum("qhk,qhd->khd", weights_low, grad_rest, preferred_element_type=jnp.float32)


def split_scaled(grad_heads, row_sum):
    grad_scaled = grad_heads.astype(jnp.float32) / row_sum[..., None]
    grad_high = grad_scaled.astype(jnp.bfloat16)
    grad_rest = (grad_scaled - grad_high.astype(jnp.float32)).astype(jnp.bfloat16)
    return (grad_high, grad_rest)


def split_blocks(arriving, query_rows):
    key_piece, value_piece = arriving
    key_count = key_piece.shape[0]
    block_rows = math.gcd(key_count, query_rows)
    block_count = key_count // block_rows
    head_count = key_piece.shape[1] // HEAD
    key_blocks = key_piece.reshape(block_count, block_rows, head_count, HEAD)
    value_blocks = value_piece.reshape(block_count, block_rows, head_count, HEAD)
    offsets = jnp.arange(block_count, dtype=jnp.int32) * block_rows
    return (key_blocks, value_blocks, offsets, block_rows)


def forward_piece(running, arriving, query_low, query_info, starts, score_scale):
    key_blocks, value_blocks, offsets, block_rows = split_blocks(arriving, query_low.shape[0])

    def forward_one_block(fold_state, block_items):
        run_max, run_sum, run_acc = fold_state
        key_block, value_block, offset = block_items
        key_index = offset + jnp.arange(block_rows, dtype=jnp.int32)
        visible = visible_pairs(query_info, key_index, starts)[:, None, :]
        scores = (
            jnp.einsum("qhd,khd->qhk", query_low, key_block, preferred_element_type=jnp.float32)
            * score_scale
        )
        block_max = jnp.max(jnp.where(visible, scores, masked_low), axis=2)
        new_max = jnp.maximum(run_max, block_max)
        weights = jnp.where(
            visible, jnp.exp(jnp.where(visible, scores - new_max[..., None], 0.0)), 0.0
        )
        factor = jnp.exp(run_max - new_max)
        run_sum = run_sum * factor + jnp.sum(weights, axis=2)
        run_acc = run_acc * factor[..., None] + jnp.einsum(
            "qhk,khd->qhd",
            weights.astype(jnp.bfloat16),
            value_block,
            preferred_element_type=jnp.float32,
        )
        return ((new_max, run_sum, run_acc), None)

    fold_state, unused = lax.scan(forward_one_block, running, (key_blocks, value_blocks, offsets))
    return fold_state


def backward_piece(
    running,
    arriving,
    query_low,
    query_info,
    starts,
    score_scale,
    row_max,
    row_sum,
    grad_heads,
    row_delta,
    grad_high,
    grad_rest,
):
    key_blocks, value_blocks, offsets, block_rows = split_blocks(arriving, query_low.shape[0])

    def backward_one_block(fold_state, block_items):
        d_query, d_keyval = fold_state
        key_block, value_block, offset = block_items
        key_index = offset + jnp.arange(block_rows, dtype=jnp.int32)
        visible = visible_pairs(query_info, key_index, starts)[:, None, :]
        scores = (
            jnp.einsum("qhd,khd->qhk", query_low, key_block, preferred_element_type=jnp.float32)
            * score_scale
        )
        weights = jnp.where(
            visible, jnp.exp(jnp.where(visible, scores - row_max[..., None], 0.0)), 0.0
        )
        probability = weights / row_sum[..., None]
        d_prob = jnp.einsum(
            "qhd,khd->qhk", grad_heads, value_block, preferred_element_type=jnp.float32
        )
        d_score = (probability * (d_prob - row_delta[..., None])).astype(jnp.bfloat16)
        d_query = (
            d_query
            + jnp.einsum("qhk,khd->qhd", d_score, key_block, preferred_element_type=jnp.float32)
            * score_scale
        )
        d_key = (
            jnp.einsum("qhk,qhd->khd", d_score, query_low, preferred_element_type=jnp.float32)
            * score_scale
        )
        d_value = value_grad(weights, grad_high, grad_rest)
        fresh = jnp.concatenate(
            [d_key.reshape(block_rows, -1), d_value.reshape(block_rows, -1)], axis=1
        )
        d_keyval = lax.dynamic_update_slice_in_dim(d_keyval, fresh, offset, 0)
        return ((d_query, d_keyval), None)

    fold_state, unused = lax.scan(backward_one_block, running, (key_blocks, value_blocks, offsets))
    return fold_state


def shards(
    tokens,
    cotangent,
    positions,
    seg_start,
    seg_parent,
    ln_gain,
    ln_bias,
    w_qkv,
    b_qkv,
    w_dense,
    b_dense,
    w_fc1,
    b_fc1,
    w_fc2,
    b_fc2,
):
    own_rows = tokens.shape[2]
    model_width = tokens.shape[3]
    ctx_rows = positions.shape[1]
    local_width = w_qkv.shape[2]
    head_count = local_width // HEAD
    score_scale = HEAD ** (-0.5)
    starts = seg_start[0]
    parents = seg_parent[0]
    query_index = lax.axis_index("ctx") * ctx_rows + jnp.arange(ctx_rows, dtype=jnp.int32)
    query_info = query_details(query_index, starts, parents)
    cosine, sine = rotary_tables(positions[0])
    contract_rows = (((0,), (0,)), ((), ()))
    contract_cols = (((1,), (1,)), ((), ()))
    residual = tokens.reshape(own_rows, model_width).astype(jnp.float32)
    centered = residual - jnp.mean(residual, axis=1, keepdims=True)
    inv_std = lax.rsqrt(jnp.mean(centered * centered, axis=1, keepdims=True) + norm_eps)
    unit_norm = centered * inv_std
    gain_wide = ln_gain.astype(jnp.float32)
    normed_low = (unit_norm * gain_wide + ln_bias.astype(jnp.float32)).astype(jnp.bfloat16)
    qkv_flat = w_qkv.reshape(model_width, 3 * local_width)
    qkv_bias = b_qkv.astype(jnp.float32).reshape(3 * local_width)
    fc1_bias = b_fc1.astype(jnp.float32)

    def inputs_from(qkv_part, hidden_part):
        qkv_heads = (qkv_part + qkv_bias).reshape(ctx_rows, 3, head_count, HEAD)
        query_low = rotate(qkv_heads[:, 0], cosine, sine).astype(jnp.bfloat16)
        key_low = rotate(qkv_heads[:, 1], cosine, sine).astype(jnp.bfloat16)
        value_low = qkv_heads[:, 2].astype(jnp.bfloat16)
        return (query_low, key_low, value_low, hidden_part + fc1_bias)

    arriving = lax.all_gather(normed_low, "tp", axis=0, tiled=True)
    projected = jnp.concatenate(
        [
            jnp.dot(arriving, qkv_flat, preferred_element_type=jnp.float32),
            jnp.dot(arriving, w_fc1, preferred_element_type=jnp.float32),
        ],
        axis=1,
    )
    query_low, key_low, value_low, hidden_pre = inputs_from(
        projected[:, : 3 * local_width], projected[:, 3 * local_width :]
    )
    start_state = (
        jnp.full((ctx_rows, head_count), masked_low, jnp.float32),
        jnp.zeros((ctx_rows, head_count), jnp.float32),
        jnp.zeros((ctx_rows, head_count, HEAD), jnp.float32),
    )

    def forward_step(query_now, running, arriving):
        return forward_piece(running, arriving, query_now, query_info, starts, score_scale)

    row_max, row_sum, attn_acc = forward_step(
        query_low,
        start_state,
        (
            lax.all_gather(key_low.reshape(ctx_rows, local_width), "ctx", axis=0, tiled=True),
            lax.all_gather(value_low.reshape(ctx_rows, local_width), "ctx", axis=0, tiled=True),
        ),
    )
    attn = attn_acc / row_sum[..., None]
    attn_low = attn.reshape(ctx_rows, local_width).astype(jnp.bfloat16)
    act_low = gelu_tanh(hidden_pre).astype(jnp.bfloat16)
    branches = lax.psum_scatter(
        (
            jnp.dot(attn_low, w_dense, preferred_element_type=jnp.float32)
            + jnp.dot(act_low, w_fc2, preferred_element_type=jnp.float32)
        ).astype(jnp.bfloat16),
        "tp",
        scatter_dimension=0,
        tiled=True,
    ).astype(jnp.float32)
    block_out = (
        (residual + branches + b_dense.astype(jnp.float32) + b_fc2.astype(jnp.float32))
        .astype(jnp.bfloat16)
        .reshape(tokens.shape)
    )
    grad_own = cotangent.reshape(own_rows, model_width)
    normed_all, grad_all = (
        lax.all_gather(normed_low, "tp", axis=0, tiled=True),
        lax.all_gather(grad_own, "tp", axis=0, tiled=True),
    )
    query_low, key_low, value_low, hidden_pre = inputs_from(
        jnp.dot(normed_all, qkv_flat, preferred_element_type=jnp.float32),
        jnp.dot(normed_all, w_fc1, preferred_element_type=jnp.float32),
    )
    row_max, row_sum, attn_acc = forward_step(
        query_low,
        start_state,
        (
            lax.all_gather(key_low.reshape(ctx_rows, local_width), "ctx", axis=0, tiled=True),
            lax.all_gather(value_low.reshape(ctx_rows, local_width), "ctx", axis=0, tiled=True),
        ),
    )
    attn = attn_acc / row_sum[..., None]
    attn_low = attn.reshape(ctx_rows, local_width).astype(jnp.bfloat16)
    act_low = gelu_tanh(hidden_pre).astype(jnp.bfloat16)
    d_attn_low = lax.dot_general(
        grad_all, w_dense, contract_cols, preferred_element_type=jnp.float32
    ).astype(jnp.bfloat16)
    d_act = lax.dot_general(grad_all, w_fc2, contract_cols, preferred_element_type=jnp.float32)
    d_hidden_low = (d_act * gelu_slope(hidden_pre)).astype(jnp.bfloat16)
    grad_heads = d_attn_low.reshape(ctx_rows, head_count, HEAD)
    row_delta = jnp.sum(grad_heads.astype(jnp.float32) * attn, axis=2)
    grad_high, grad_rest = split_scaled(grad_heads, row_sum)
    buffer_rows = ctx_rows * lax.axis_size("ctx")
    back_state = (
        jnp.zeros((ctx_rows, head_count, HEAD), jnp.float32),
        jnp.zeros((buffer_rows, 2 * local_width), jnp.float32),
    )
    d_query, d_keyval = backward_piece(
        back_state,
        (
            lax.all_gather(key_low.reshape(ctx_rows, local_width), "ctx", axis=0, tiled=True),
            lax.all_gather(value_low.reshape(ctx_rows, local_width), "ctx", axis=0, tiled=True),
        ),
        query_low,
        query_info,
        starts,
        score_scale,
        row_max,
        row_sum,
        grad_heads,
        row_delta,
        grad_high,
        grad_rest,
    )
    own_keyval = lax.psum_scatter(
        d_keyval.astype(jnp.bfloat16), "ctx", scatter_dimension=0, tiled=True
    ).astype(jnp.float32)
    d_key = own_keyval[:, :local_width].reshape(ctx_rows, head_count, HEAD)
    d_qkv_low = jnp.concatenate(
        [
            rotate_back(d_query, cosine, sine).reshape(ctx_rows, local_width),
            rotate_back(d_key, cosine, sine).reshape(ctx_rows, local_width),
            own_keyval[:, local_width:],
        ],
        axis=1,
    ).astype(jnp.bfloat16)
    d_normed = lax.psum_scatter(
        (
            lax.dot_general(d_qkv_low, qkv_flat, contract_cols, preferred_element_type=jnp.float32)
            + lax.dot_general(
                d_hidden_low, w_fc1, contract_cols, preferred_element_type=jnp.float32
            )
        ).astype(jnp.bfloat16),
        "tp",
        scatter_dimension=0,
        tiled=True,
    ).astype(jnp.float32)
    scaled = d_normed * gain_wide
    d_tokens = grad_own.astype(jnp.float32) + inv_std * (
        scaled
        - jnp.mean(scaled, axis=1, keepdims=True)
        - unit_norm * jnp.mean(scaled * unit_norm, axis=1, keepdims=True)
    )
    grad_qkv = lax.dot_general(
        normed_all, d_qkv_low, contract_rows, preferred_element_type=jnp.float32
    ).reshape(model_width, 3, local_width)
    grad_qkv_bias = jnp.sum(d_qkv_low.astype(jnp.float32), axis=0).reshape(3, local_width)
    grad_dense = lax.dot_general(
        attn_low, grad_all, contract_rows, preferred_element_type=jnp.float32
    )
    grad_fc1 = lax.dot_general(
        normed_all, d_hidden_low, contract_rows, preferred_element_type=jnp.float32
    )
    grad_fc1_bias = jnp.sum(d_hidden_low.astype(jnp.float32), axis=0)
    grad_fc2 = lax.dot_general(act_low, grad_all, contract_rows, preferred_element_type=jnp.float32)
    sum_qkv, sum_qkv_bias, sum_dense, sum_fc1, sum_fc1_bias, sum_fc2 = (
        lax.psum_scatter(grad_qkv, ("ctx", "rep"), scatter_dimension=0, tiled=True),
        lax.psum_scatter(grad_qkv_bias, ("ctx", "rep"), scatter_dimension=1, tiled=True),
        lax.psum_scatter(grad_dense, ("ctx", "rep"), scatter_dimension=0, tiled=True),
        lax.psum_scatter(grad_fc1, ("ctx", "rep"), scatter_dimension=0, tiled=True),
        lax.psum_scatter(grad_fc1_bias, ("ctx", "rep"), scatter_dimension=0, tiled=True),
        lax.psum_scatter(grad_fc2, ("ctx", "rep"), scatter_dimension=0, tiled=True),
    )
    gain_grad, bias_grad, out_bias_grad = (
        lax.psum_scatter(
            jnp.sum(d_normed * unit_norm, axis=0),
            ("tp", "ctx", "rep"),
            scatter_dimension=0,
            tiled=True,
        ),
        lax.psum_scatter(
            jnp.sum(d_normed, axis=0), ("tp", "ctx", "rep"), scatter_dimension=0, tiled=True
        ),
        lax.psum_scatter(
            jnp.sum(grad_own.astype(jnp.float32), axis=0),
            ("tp", "ctx", "rep"),
            scatter_dimension=0,
            tiled=True,
        ),
    )
    return (
        block_out,
        d_tokens.reshape(tokens.shape),
        gain_grad,
        bias_grad,
        sum_qkv,
        sum_qkv_bias,
        sum_dense,
        out_bias_grad,
        sum_fc1,
        sum_fc1_bias,
        sum_fc2,
        out_bias_grad,
    )


def solution(mesh):
    return jax.shard_map(
        shards,
        mesh=mesh,
        in_specs=(
            P("rep", "ctx", "tp", None),
            P("rep", "ctx", "tp", None),
            P("rep", "ctx"),
            P("rep", None),
            P("rep", None),
            P(),
            P(),
            P(None, None, "tp"),
            P(None, "tp"),
            P("tp", None),
            P(),
            P(None, "tp"),
            P("tp"),
            P("tp", None),
            P(),
        ),
        out_specs=(
            P("rep", "ctx", "tp", None),
            P("rep", "ctx", "tp", None),
            P(("tp", "ctx", "rep")),
            P(("tp", "ctx", "rep")),
            P(("ctx", "rep"), None, "tp"),
            P(None, ("tp", "ctx", "rep")),
            P(("tp", "ctx", "rep"), None),
            P(("tp", "ctx", "rep")),
            P(("ctx", "rep"), "tp"),
            P(("tp", "ctx", "rep")),
            P(("tp", "ctx", "rep"), None),
            P(("tp", "ctx", "rep")),
        ),
        check_vma=False,
    )
```

profile of v0, /device:TPU:0, one launch (start us, length us, event | category | flops | bytes accessed | tf_op | source)
XLA Modules:
  0.0 1571.0 jit_solution(13662690220208967005)
XLA Ops:
  14.7 17.0 %copy.74 = bf16[2048,3,1024]{0,2,1:T(8,128)(2,1)} copy(bf16[2048,3,1024]{2,0,1:T(8,128)(2,1)} %param.26) | data formatting | bytes 25165824 | tf_op args[7]
  32.0 9.7 all-gather.6.cloned.1.call-done
  41.7 11.4 convolution_add_fusion.2
  73.0 23.8 %all-gather.8.cloned.1.call-done = bf16[1344,1024]{1,0:T(8,128)(2,1)} async-done(((bf16[336,1024]{1,0:T(8,128)(2,1)}), bf16[1344,1024]{1,0:T(8,128)(2,1)}) %all-gather.8.cloned.1.call-update) | async-done | bytes 2752528 | tf_op jit(solution)/shard_map/all_gather | solution.py:278
  96.8 8.0 reshape.444
  104.8 8.0 copy.80
  112.8 12.3 all-gather.10.cloned.1.call-done
  125.1 8.0 reshape.445
  133.1 7.9 copy.81
  141.0 73.1 %while.38 = (s32[]{:T(128)}, f32[336,16]{0,1:T(8,128)S(1)}, f32[336,16]{0,1:T(8,128)S(1)}, f32[336,16,64]{0,2,1:T(8,128)}, s32[1,13]{1,0:T(1,128)S(1)}, /*index=...) while((s32[]{:T(128)}, f32[336,16]{0,1:T(8,128)S(1)}, ...), condition=%wide.region_9.10_spmd.clone, body=%wide.region_5.9_spmd.clone.sunk | while | flops 487767488 | bytes 56600572 | solution.py:150
  142.6 5.9 fusion.138
  160.5 5.9 fusion.138
  220.5 140.5 %while.39 = (s32[]{:T(128)}, f32[336,16,64]{0,2,1:T(8,128)}, bf16[1344,2048]{1,0:T(8,128)(2,1)}, bf16[4,336,16,64]{1,3,2,0:T(8,128)(2,1)}, s32[1,13]{1,0:T(1,128...) while((s32[]{:T(128)}, f32[336,16,64]{0,2,1:T(8,128)}, ...), condition=%wide.region_14.15_spmd.clone, body=%wide.region_12.14_spmd.clone.sunk | while | flops 1425745152 | bytes 87232128 | solution.py:203
  243.7 7.6 dynamic_update_slice.8
  278.7 7.6 dynamic_update_slice.8
  313.8 7.6 dynamic_update_slice.8
  348.9 7.5 dynamic_update_slice.8
  362.4 10.3 convolution_add_fusion.1
  372.7 15.4 convert_reduce_fusion.2
  388.1 11.5 fusion.88
  399.7 14.7 reduce-scatter.25.cloned.1.call-done
  423.6 13.9 add_convert_fusion
  437.6 12.2 fusion.86
  452.7 16.4 %fusion.85 = f32[2048,3072]{0,1:T(8,128)} fusion(bf16[336,2048]{1,0:T(8,128)(2,1)} %all-gather.6.cloned.1.call-done, bf16[336,1024]{0,1:T(8,128)(2,1)S(1)} %copy.102, bf16[336,1024]{0,1:T(8,128)(2,1)S(1)} %bitcast.250, bf16[336,1024]{0,1:T(8,128)(2,1)S(1)} %bitcast.247), kind=kOutput, calls=%fused_computation.155 | convolution fusion | flops 4234051584 | bytes 28606464 | tf_op jit(solution)/shard_map/dot_general | solution.py:378
  477.4 17.5 %fusion.89 = f32[2048,4096]{1,0:T(8,128)} fusion(bf16[336,2048]{1,0:T(8,128)(2,1)S(1)} %copy-done.8, bf16[336,4096]{1,0:T(8,128)(2,1)} %get-tuple-element.782), kind=kOutput, calls=%fused_computation.159 | convolution fusion | flops 5637144576 | bytes 37683200 | tf_op jit(solution)/shard_map/dot_general | solution.py:385
  494.9 18.6 %fusion.72 = f32[4096,2048]{1,0:T(8,128)} fusion(bf16[1,1,336,2048]{3,2,1,0:T(8,128)(2,1)S(1)} %copy-done.11, f32[336,4096]{1,0:T(8,128)} %copy-done.6), kind=kOutput, calls=%fused_computation.112 | convolution fusion | flops 5649530880 | bytes 40435712 | tf_op jit(solution)/shard_map/dot_general | solution.py:389
  515.6 60.6 %all-reduce.3 = f32[4096]{0:T(1024)S(1)} all-reduce(f32[4096]{0:T(1024)S(1)} %get-tuple-element.781), channel_id=13, replica_groups=mesh['tp'=2,'ctx'=4,'rep'=4] {'ctx','rep'}, use_global_device_ids=true, to_apply=%region_31.32.clone | all-reduce | flops 4096 | bytes 32768
  580.1 43.6 %all-reduce.4 = (f32[2048]{0:T(1024)S(1)}, f32[2048]{0:T(1024)S(1)}, f32[2048]{0:T(1024)S(1)}) all-reduce(f32[2048]{0:T(1024)S(1)} %get-tuple-element.680, f32[2048]{0:T(1024)S(1)} %get-tuple-element.683, f32[2048]{0:T(1024)S(1)} %convert_reduce_fusion.5), channel_id=6, replica_groups=mesh['tp'=2,'ctx'=4,'rep'=4] {'tp','ctx','rep'}, use_global_device_ids=true, to_apply=%region_20.21.clone | all-reduce | flops 6144 | bytes 49152
  628.4 152.9 %reduce-scatter.17.cloned.1.call-done = f32[128,3,1024]{0,2,1:T(8,128)} async-done(((f32[2048,3,1024]{0,2,1:T(8,128)}), f32[128,3,1024]{0,2,1:T(8,128)}) %reduce-scatter.17.cloned.1.call-update) | async-done | bytes 1572880 | tf_op jit(solution)/shard_map/reduce_scatter | solution.py:391
  784.3 105.2 %reduce-scatter.19.cloned.1.call-done = f32[64,2048]{1,0:T(8,128)} async-done(((f32[1024,2048]{1,0:T(8,128)}), f32[64,2048]{1,0:T(8,128)}) %reduce-scatter.19.cloned.1.call-update) | async-done | bytes 524304 | tf_op jit(solution)/shard_map/reduce_scatter | solution.py:393
  889.5 337.4 %reduce-scatter.21.cloned.1.call-done = f32[128,4096]{1,0:T(8,128)} async-done(((f32[2048,4096]{1,0:T(8,128)}), f32[128,4096]{1,0:T(8,128)}) %reduce-scatter.21.cloned.1.call-update) | async-done | bytes 2097168 | tf_op jit(solution)/shard_map/reduce_scatter | solution.py:394
  1226.9 336.5 %reduce-scatter.23.cloned.1.call-done = f32[256,2048]{1,0:T(8,128)} async-done(((f32[4096,2048]{1,0:T(8,128)}), f32[256,2048]{1,0:T(8,128)}) %reduce-scatter.23.cloned.1.call-update) | async-done | bytes 2097168 | tf_op jit(solution)/shard_map/reduce_scatter | solution.py:396
  (278 shorter events, 231.6 us)
Async XLA Ops:
  7.2 34.6 %all-gather.6.cloned.1.call-start = ((), (), s32[]{:S(2)}) async-start(), calls=%async_computation.8 | async-start | bytes 2064384 | tf_op jit(solution)/shard_map/all_gather | solution.py:254
  13.9 54.4 %all-gather.12.cloned.1.call-start = ((), (), s32[]{:S(2)}) async-start(), calls=%async_computation.17 | async-start | bytes 2064384 | tf_op jit(solution)/shard_map/all_gather | solution.py:302
  14.6 82.2 %all-gather.8.cloned.1.call-start = ((), (), s32[]{:S(2)}) async-start(), calls=%async_computation.9 | async-start | bytes 3440640 | tf_op jit(solution)/shard_map/all_gather | solution.py:278
  14.7 17.1 %copy-start.26 = (bf16[3,1024]{1,0:T(4,128)(2,1)S(1)}, bf16[3,1024]{1,0:T(4,128)(2,1)}, u32[]{:S(2)}) copy-start(bf16[3,1024]{1,0:T(4,128)(2,1)} %param.27) | copy-start | bytes 18436
  14.7 17.1 %copy-start.30 = (s32[1,336]{1,0:T(1,128)S(1)}, s32[1,336]{1,0:T(1,128)}, u32[]{:S(2)}) copy-start(s32[1,336]{1,0:T(1,128)} %param.21) | copy-start | bytes 4036
  32.0 29.1 %copy-start.14 = (f32[336,16]{0,1:T(8,128)}, f32[336,16]{0,1:T(8,128)S(1)}, u32[]{:S(2)}) copy-start(f32[336,16]{0,1:T(8,128)S(1)} %get-tuple-element.779) | copy-start | bytes 64516
  32.0 29.1 %copy-start.16 = (f32[336,16]{0,1:T(8,128)}, f32[336,16]{0,1:T(8,128)S(1)}, u32[]{:S(2)}) copy-start(f32[336,16]{0,1:T(8,128)S(1)} %get-tuple-element.780) | copy-start | bytes 64516
  63.3 61.8 %all-gather.10.cloned.1.call-start = ((), (), s32[]{:S(2)}) async-start(), calls=%async_computation.10 | async-start | bytes 3440640 | tf_op jit(solution)/shard_map/all_gather | solution.py:279
  66.0 348.4 %reduce-scatter.25.cloned.1.call-start = ((), (), s32[]{:S(2)}) async-start(), calls=%async_computation.18 | async-start | bytes 6881280
  241.6 9.6 copy-start.2
  276.7 9.7 copy-start.2
  311.8 9.7 copy-start.2
  346.9 9.6 copy-start.2
  361.1 215.7 %reduce-scatter.27.cloned.1.call-start = ((), (), s32[]{:S(2)}) async-start(), calls=%async_computation.19 | async-start | bytes 557056
  362.4 10.3 copy-start.10
  372.7 15.4 copy-start.6
  388.1 11.5 copy-start.4
  399.7 19.3 %copy-start.15 = (f32[336,16]{0,1:T(8,128)S(1)}, f32[336,16]{0,1:T(8,128)}, u32[]{:S(2)}) copy-start(f32[336,16]{0,1:T(8,128)} %copy-done.14) | copy-start | bytes 64516
  399.7 19.3 %copy-start.17 = (f32[336,16]{0,1:T(8,128)S(1)}, f32[336,16]{0,1:T(8,128)}, u32[]{:S(2)}) copy-start(f32[336,16]{0,1:T(8,128)} %copy-done.16) | copy-start | bytes 64516
  423.6 154.7 %reduce-scatter.15.cloned.1.call-start = ((), (), s32[]{:S(2)}) async-start(), calls=%async_computation.12 | async-start | bytes 2064384 | tf_op jit(solution)/shard_map/reduce_scatter | solution.py:361
  437.5 12.3 copy-start.12
  437.6 187.4 %reduce-scatter.13.cloned.1.call-start = ((), (), s32[]{:S(2)}) async-start(), calls=%async_computation.11 | async-start | bytes 2064384 | tf_op jit(solution)/shard_map/reduce_scatter | solution.py:285
  437.6 12.3 copy-start.31
  452.6 328.7 %reduce-scatter.17.cloned.1.call-start = ((), (), s32[]{:S(2)}) async-start(), calls=%async_computation.13 | async-start | bytes 26738688 | tf_op jit(solution)/shard_map/reduce_scatter | solution.py:391
  469.1 420.4 %reduce-scatter.19.cloned.1.call-start = ((), (), s32[]{:S(2)}) async-start(), calls=%async_computation.14 | async-start | bytes 8912896 | tf_op jit(solution)/shard_map/reduce_scatter | solution.py:393
  476.1 750.8 %reduce-scatter.21.cloned.1.call-start = ((), (), s32[]{:S(2)}) async-start(), calls=%async_computation.15 | async-start | bytes 35651584 | tf_op jit(solution)/shard_map/reduce_scatter | solution.py:394
  494.9 1068.5 %reduce-scatter.23.cloned.1.call-start = ((), (), s32[]{:S(2)}) async-start(), calls=%async_computation.16 | async-start | bytes 35651584 | tf_op jit(solution)/shard_map/reduce_scatter | solution.py:396
  513.5 64.7 %copy-start.5 = (bf16[1,1,168,2048]{3,2,1,0:T(8,128)(2,1)S(1)}, bf16[1,1,168,2048]{3,2,1,0:T(8,128)(2,1)}, u32[]{:S(2)}) copy-start(bf16[1,1,168,2048]{3,2,1,0:T(8,128)(2,1)} %param.19) | copy-start | bytes 2064388
  513.6 64.7 %copy-start.19 = (f32[2048]{0:T(1024)S(1)}, f32[2048]{0:T(1024)}, u32[]{:S(2)}) copy-start(f32[2048]{0:T(1024)} %copy-done.18) | copy-start | bytes 24580
  513.6 64.7 %copy-start.22 = (f32[168]{0:T(256)S(1)}, f32[168]{0:T(256)}, u32[]{:S(2)}) copy-start(f32[168]{0:T(256)} %copy-done.21) | copy-start | bytes 2020
  513.6 64.7 %copy-start.24 = (f32[168]{0:T(256)S(1)}, f32[168]{0:T(256)}, u32[]{:S(2)}) copy-start(f32[168]{0:T(256)} %copy-done.23) | copy-start | bytes 2020
  623.8 939.6 %copy-start.33 = (f32[64]{0:T(128)}, f32[64]{0:T(128)S(1)}, u32[]{:S(2)}) copy-start(f32[64]{0:T(128)S(1)} %dynamic-slice.2) | copy-start | bytes 772
  (26 other events, 64.1 us)
Sparse Core Ops, SparseCore 0:
  14.0 27.6 all-gather.5
  43.3 24.9 all-gather.11
  70.4 26.2 all-gather.7
  98.8 26.2 all-gather.9
  361.2 53.1 reduce-scatter.24
  423.7 55.8 reduce-scatter.26
  482.4 22.9 reduce-scatter.14
  508.3 23.9 reduce-scatter.12
  536.3 244.8 reduce-scatter.16
  785.8 103.6 reduce-scatter.18
  894.3 332.4 reduce-scatter.20
  1231.6 331.7 reduce-scatter.22
where the time goes:
time: 1580 us; the launch traced here: 1570 us
  waiting for transfers between devices  995 us (63%)
  matrix products  260 us (16%)
  local copies, waits for them, and re-layouts  140 us (9%)
  blocking collectives  104 us (7%)
  other arithmetic  47 us (3%)
    reduce_scatter x1, waiting for transfers between devices, shards(): lax.psum_scatter(grad_fc1, ('ctx', 'rep'), scatter_dimension=0, tiled=True)  337 us
    reduce_scatter x1, waiting for transfers between devices, shards(): lax.psum_scatter(grad_fc2, ('ctx', 'rep'), scatter_dimension=0, tiled=True)  336 us
    reduce_scatter x1, waiting for transfers between devices, shards(): lax.psum_scatter(grad_qkv, ('ctx', 'rep'), scatter_dimension=0, tiled=True)  153 us
    reduce_scatter x1, waiting for transfers between devices, shards(): lax.psum_scatter(grad_dense, ('ctx', 'rep'), scatter_dimension=0, tiled=T...  105 us
    unnamed x2, blocking collectives  104 us
    unnamed x74, local copies, waits for them, and re-layouts  47.7 us
    dynamic_update_slice x8, local copies, waits for them, and re-layouts, backward_one_block(): d_keyval = lax.dynamic_update_slice_in_dim(d_keyval, fresh, offset, 0)  36.6 us
  transfers between devices with their start and end apart: 12, of which 9 were waited for; matrix products, arithmetic and copies ran while one was open for 13% of the time, Pallas kernels for 0%

commit v1 on v0

v1 whole, which is shorter than its diff:
```python
import functools

import jax
import jax.numpy as jnp
from jax import lax
from jax.experimental import pallas as pl
from jax.experimental.pallas import tpu as pltpu
from jax.sharding import PartitionSpec as P

HEAD = 64
ROT = 32
LANES = 128


norm_eps = 1e-05
masked_low = -1e30
gelu_root = 0.7978845608028654
gelu_cube = 0.044715
bf16 = jnp.bfloat16
NT = (((1,), (1,)), ((), ()))
NN = (((1,), (0,)), ((), ()))
TN = (((0,), (0,)), ((), ()))


def gelu_tanh(values):
    return (
        0.5 * values * (1.0 + jnp.tanh(gelu_root * (values + gelu_cube * values * values * values)))
    )


def gelu_slope(values):
    tangent = jnp.tanh(gelu_root * (values + gelu_cube * values * values * values))
    return 0.5 * (1.0 + tangent) + 0.5 * values * (1.0 - tangent * tangent) * gelu_root * (
        1.0 + 3.0 * gelu_cube * values * values
    )


def dot32(lhs, rhs, dims):
    return lax.dot_general(lhs, rhs, dims, preferred_element_type=jnp.float32)


def rotary_tables(rows, starts, parents):
    segs = starts.shape[0]
    index = jnp.arange(rows, dtype=jnp.int32)
    place = index
    for seg in range(1, segs):
        up = parents[seg]
        depth = starts[1] + jnp.where(up == 0, 0, starts[up + 1] - starts[up])
        place = jnp.where(index >= starts[seg], index - starts[seg] + depth, place)
    freq_index = jnp.arange(ROT // 2, dtype=jnp.float32)
    inverse = jnp.power(10000.0, -2.0 * freq_index / ROT)
    angles = place.astype(jnp.float32)[:, None] * inverse[None, :]
    cosine, sine = jnp.cos(angles), jnp.sin(angles)
    half = ROT // 2
    ones = jnp.ones((rows, HEAD - ROT), jnp.float32)
    zeros = jnp.zeros((rows, half), jnp.float32)
    rest = jnp.zeros((rows, HEAD - ROT), jnp.float32)
    copies = (1, LANES // HEAD)
    return (
        jnp.tile(jnp.concatenate([cosine, cosine, ones], axis=1), copies),
        jnp.tile(jnp.concatenate([-sine, zeros, rest], axis=1), copies),
        jnp.tile(jnp.concatenate([zeros, sine, rest], axis=1), copies),
    )

def tree_attention_body(
    heads, width, tokens, q_rows, k_rows,
    starts, parents, pre_ref, grad_ref, cos_ref, low_ref, high_ref,
    attn_ref, dqkv_ref,
    key_all, val_all, key_tr, val_tr, d_key, d_val, scores, key_bits, dq_acc, out_acc,
    block_bits, chosen,
):
    step = pl.program_id(0)
    segs = starts.shape[0]
    stack = heads * q_rows
    per_key = k_rows // q_rows
    key_blocks = key_all.shape[0]
    tail_rows = tokens % q_rows
    last = pl.num_programs(0) - 1
    far = key_blocks * k_rows

    def seg_end(seg):
        return starts[seg + 1] if seg + 1 < segs else far

    def seen_bits(seg):
        up_one = parents[seg]
        up_two = parents[up_one]
        one = jnp.int32(1)
        return (
            lax.shift_left(one, jnp.int32(seg))
            | lax.shift_left(one, up_one)
            | lax.shift_left(one, up_two)
        )

    @pl.when(step == 0)
    def _():
        key_all[...] = jnp.zeros_like(key_all)
        val_all[...] = jnp.zeros_like(val_all)
        key_tr[...] = jnp.zeros_like(key_tr)
        val_tr[...] = jnp.zeros_like(val_tr)
        d_key[...] = jnp.zeros_like(d_key)
        d_val[...] = jnp.zeros_like(d_val)
        for block in range(key_blocks):
            index = block * k_rows + lax.broadcasted_iota(jnp.int32, (k_rows, q_rows), 0)
            bits = jnp.full((k_rows, q_rows), 1, jnp.int32)
            held = jnp.int32(0)
            for seg in range(segs):
                if seg:
                    bits = jnp.where(index >= starts[seg], jnp.int32(1 << seg), bits)
                inside = (starts[seg] < (block + 1) * k_rows) & (seg_end(seg) > block * k_rows)
                held = held | jnp.where(inside, jnp.int32(1 << seg), jnp.int32(0))
            key_bits[block] = bits
            block_bits[block] = held

    row_start = step * q_rows
    query_at = row_start + lax.broadcasted_iota(jnp.int32, (1, q_rows), 1)
    seen = jnp.full((1, q_rows), 1, jnp.int32)
    seen_any = jnp.int32(0)
    for seg in range(segs):
        bits = seen_bits(seg)
        if seg:
            seen = jnp.where(query_at >= starts[seg], bits, seen)
        inside = (starts[seg] < row_start + q_rows) & (seg_end(seg) > row_start)
        seen_any = seen_any | jnp.where(inside, bits, jnp.int32(0))

    def pick(block, count):
        wanted = (block_bits[block] & seen_any) != 0

        @pl.when(wanted)
        def _():
            chosen[count] = block

        return count + wanted.astype(jnp.int32)

    picked = lax.fori_loop(0, (step + per_key) // per_key, pick, jnp.int32(0))

    row_at = row_start + lax.broadcasted_iota(jnp.int32, (q_rows, LANES), 0)
    real = row_at < tokens
    cos = cos_ref[pl.ds(pl.multiple_of(row_start, q_rows), q_rows), :]
    low = low_ref[pl.ds(pl.multiple_of(row_start, q_rows), q_rows), :]
    high = high_ref[pl.ds(pl.multiple_of(row_start, q_rows), q_rows), :]

    def turn(values, sign, cos, low, high):
        return values * cos + sign * (
            pltpu.roll(values, LANES - ROT // 2, 1) * low + pltpu.roll(values, ROT // 2, 1) * high
        )

    queries, grads = [], []
    in_block = step // per_key
    in_rows = pl.ds(pl.multiple_of((step % per_key) * q_rows, q_rows), q_rows)
    for part in range(width // LANES):
        lanes = slice(part * LANES, (part + 1) * LANES)

        def piece(which):
            at = which * width + part * LANES
            return jnp.where(real, pre_ref[:, at : at + LANES], 0.0)

        queries.append(turn(piece(0), 1.0, cos, low, high).astype(jnp.bfloat16))
        key_part = turn(piece(1), 1.0, cos, low, high)
        val_part = piece(2)
        key_all[in_block, in_rows, lanes] = key_part.astype(jnp.bfloat16)
        val_all[in_block, in_rows, lanes] = val_part.astype(jnp.bfloat16)
        key_tr[step, lanes, :] = key_part.T.astype(jnp.bfloat16)
        val_tr[step, lanes, :] = val_part.T.astype(jnp.bfloat16)
        grads.append(jnp.where(real, grad_ref[:, lanes].astype(jnp.float32), 0.0))
    query = jnp.concatenate(queries, axis=1) * jnp.bfloat16(HEAD ** (-0.5))
    grad = jnp.concatenate(grads, axis=1)
    grad_tr = jnp.concatenate([part.T for part in grads], axis=0)
    lane_head = lax.broadcasted_iota(jnp.int32, (q_rows, width), 1) // HEAD
    query_stack = jnp.concatenate(
        [jnp.where(lane_head == head, query, jnp.bfloat16(0)) for head in range(heads)], axis=0
    )
    grad_low = grad.astype(jnp.bfloat16)
    grad_stack = jnp.concatenate(
        [jnp.where(lane_head == head, grad_low, jnp.bfloat16(0)) for head in range(heads)], axis=0
    )

    def transposed(cube, block):
        return jnp.concatenate([cube[block * per_key + at] for at in range(per_key)], axis=1)

    def score_block(at, row_max):
        block = chosen[at]
        raw = dot32(key_all[block], query_stack, NT)
        key_at = block * k_rows + lax.broadcasted_iota(jnp.int32, (k_rows, q_rows), 0)
        visible = ((key_bits[block] & seen) != 0) & (key_at <= query_at)
        for head in range(heads):
            lanes = slice(head * q_rows, (head + 1) * q_rows)
            scores[at, :, lanes] = jnp.where(visible, raw[:, lanes], masked_low)
        return jnp.maximum(row_max, jnp.max(scores[at], axis=0, keepdims=True))

    row_max = lax.fori_loop(
        0, picked, score_block, jnp.full((1, stack), masked_low, jnp.float32)
    )
    out_acc[...] = jnp.zeros_like(out_acc)
    dq_acc[...] = jnp.zeros_like(dq_acc)

    def weight_block(at, row_sum):
        block = chosen[at]
        weights = jnp.exp(scores[at] - row_max)
        scores[at] = weights
        out_acc[...] += dot32(transposed(val_tr, block), weights.astype(jnp.bfloat16), NN)
        return row_sum + jnp.sum(weights, axis=0, keepdims=True)

    row_sum = lax.fori_loop(0, picked, weight_block, jnp.zeros((1, stack), jnp.float32))
    inverse = 1.0 / row_sum
    outs, deltas = [], []
    for head in range(heads):
        lanes = slice(head * q_rows, (head + 1) * q_rows)
        rows = slice(head * HEAD, (head + 1) * HEAD)
        out_head = out_acc[rows, lanes] * inverse[:, lanes]
        outs.append(out_head)
        deltas.append(jnp.sum(out_head * grad_tr[rows], axis=0, keepdims=True))
    if heads * HEAD < width:
        outs.append(jnp.zeros((width - heads * HEAD, q_rows), jnp.float32))
    attn_ref[...] = jnp.concatenate(outs, axis=0).T.astype(jnp.bfloat16)
    delta = jnp.concatenate(deltas, axis=1)

    def back_block(at, unused):
        block = chosen[at]
        prob = scores[at] * inverse
        d_prob = dot32(val_all[block], grad_stack, NT)
        d_score = (prob * (d_prob - delta)).astype(jnp.bfloat16)
        dq_acc[...] += dot32(transposed(key_tr, block), d_score, NN)
        d_key[block] += dot32(d_score, query_stack, NN)
        d_val[block] += dot32(prob.astype(jnp.bfloat16), grad_stack, NN)
        return unused

    lax.fori_loop(0, picked, back_block, 0)

    def store_rows(block, which, values):
        lanes = slice(which, which + values.shape[1])

        def full():
            dqkv_ref[pl.ds(pl.multiple_of(block * q_rows, q_rows), q_rows), lanes] = values

        def short():
            dqkv_ref[tokens - tail_rows :, lanes] = values[:tail_rows]

        if not tail_rows:
            full()
        else:
            pl.when(block < last)(full)
            pl.when(block == last)(short)

    dq_heads = [
        dq_acc[head * HEAD : (head + 1) * HEAD, head * q_rows : (head + 1) * q_rows]
        for head in range(heads)
    ]
    if heads * HEAD < width:
        dq_heads.append(jnp.zeros((width - heads * HEAD, q_rows), jnp.float32))
    dq = jnp.concatenate(dq_heads, axis=0).T * (HEAD ** (-0.5))
    for part in range(width // LANES):
        turned = turn(dq[:, part * LANES : (part + 1) * LANES], -1.0, cos, low, high)
        store_rows(step, part * LANES, turned.astype(jnp.bfloat16))

    @pl.when(step == last)
    def _():
        def finish(block, unused):
            rows = pl.ds(pl.multiple_of(block * q_rows, q_rows), q_rows)
            from_rows = pl.ds(pl.multiple_of((block % per_key) * q_rows, q_rows), q_rows)
            for part in range(width // LANES):
                lanes = slice(part * LANES, (part + 1) * LANES)
                turned = turn(
                    d_key[block // per_key, from_rows, lanes],
                    -1.0, cos_ref[rows, :], low_ref[rows, :], high_ref[rows, :],
                )
                store_rows(block, width + part * LANES, turned.astype(jnp.bfloat16))
                store_rows(
                    block,
                    2 * width + part * LANES,
                    d_val[block // per_key, from_rows, lanes].astype(jnp.bfloat16),
                )
            return unused

        lax.fori_loop(0, last + 1, finish, 0)


def tree_attention(starts, parents, pre, grad, tables, heads, width, q_rows=128, k_rows=256):
    tokens = pre.shape[0]
    q_blocks = pl.cdiv(tokens, q_rows)
    per_key = k_rows // q_rows
    key_blocks = pl.cdiv(q_blocks, per_key)
    stack = heads * q_rows
    pairs = q_blocks * (q_blocks + 1) // 2 * q_rows * q_rows
    whole = lambda shape: pl.BlockSpec(shape, lambda i, *s: (0, 0))
    bf = jnp.bfloat16
    return pl.pallas_call(
        functools.partial(tree_attention_body, heads, width, tokens, q_rows, k_rows),
        out_shape=(
            jax.ShapeDtypeStruct((tokens, width), bf),
            jax.ShapeDtypeStruct((tokens, 3 * width), bf),
        ),
        grid_spec=pltpu.PrefetchScalarGridSpec(
            num_scalar_prefetch=2,
            grid=(q_blocks,),
            in_specs=[
                pl.BlockSpec((q_rows, 3 * width), lambda i, *s: (i, 0)),
                pl.BlockSpec((q_rows, width), lambda i, *s: (i, 0)),
            ]
            + [whole(tables[0].shape)] * 3,
            out_specs=[
                pl.BlockSpec((q_rows, width), lambda i, *s: (i, 0)),
                whole((tokens, 3 * width)),
            ],
            scratch_shapes=[
                pltpu.VMEM((key_blocks, k_rows, width), bf),
                pltpu.VMEM((key_blocks, k_rows, width), bf),
                pltpu.VMEM((key_blocks * per_key, width, q_rows), bf),
                pltpu.VMEM((key_blocks * per_key, width, q_rows), bf),
                pltpu.VMEM((key_blocks, k_rows, width), jnp.float32),
                pltpu.VMEM((key_blocks, k_rows, width), jnp.float32),
                pltpu.VMEM((key_blocks, k_rows, stack), jnp.float32),
                pltpu.VMEM((key_blocks, k_rows, q_rows), jnp.int32),
                pltpu.VMEM((width, stack), jnp.float32),
                pltpu.VMEM((width, stack), jnp.float32),
                pltpu.SMEM((key_blocks,), jnp.int32),
                pltpu.SMEM((key_blocks,), jnp.int32),
            ],
        ),
        compiler_params=pltpu.CompilerParams(
            dimension_semantics=("arbitrary",), vmem_limit_bytes=60 << 20
        ),
        cost_estimate=pl.CostEstimate(
            flops=12 * pairs * heads * width,
            bytes_accessed=tokens * width * 24,
            transcendentals=pairs * heads,
        ),
        name="tree_attention",
    )(starts, parents, pre, grad, *tables)


def shards(
    tokens,
    cotangent,
    positions,
    seg_start,
    seg_parent,
    ln_gain,
    ln_bias,
    w_qkv,
    b_qkv,
    w_dense,
    b_dense,
    w_fc1,
    b_fc1,
    w_fc2,
    b_fc2,
):
    own_rows, model_width = tokens.shape[2:]
    ctx = lax.axis_size("ctx")
    rep = lax.axis_size("rep")
    mine = lax.axis_index("ctx")
    tree = own_rows * ctx * lax.axis_size("tp")
    head_lanes = w_qkv.shape[2] // ctx
    heads = head_lanes // HEAD
    width = max(head_lanes, LANES)
    units = w_fc1.shape[1] // ctx
    row_split = model_width // (ctx * rep)
    starts = seg_start[0]
    parents = seg_parent[0]

    residual = tokens.reshape(own_rows, model_width).astype(jnp.float32)
    centered = residual - jnp.mean(residual, axis=1, keepdims=True)
    inv_std = lax.rsqrt(jnp.mean(centered * centered, axis=1, keepdims=True) + norm_eps)
    unit_norm = centered * inv_std
    gain_wide = ln_gain.astype(jnp.float32)
    normed_own = (unit_norm * gain_wide + ln_bias.astype(jnp.float32)).astype(bf16)
    grad_own = cotangent.reshape(own_rows, model_width)
    normed = lax.all_gather(normed_own, ("ctx", "tp"), axis=0, tiled=True)
    grad = lax.all_gather(grad_own, ("ctx", "tp"), axis=0, tiled=True)

    def own_heads(array, axis):
        part = lax.dynamic_slice_in_dim(array, mine * head_lanes, head_lanes, axis)
        if width > head_lanes:
            pads = [(0, 0)] * part.ndim
            pads[axis] = (0, width - head_lanes)
            part = jnp.pad(part, pads)
        return part

    qkv_parts = own_heads(jnp.transpose(w_qkv, (1, 0, 2)), 2)
    qkv_own = jnp.concatenate([qkv_parts[0], qkv_parts[1], qkv_parts[2]], axis=1)
    qkv_bias = own_heads(b_qkv, 1).reshape(3 * width).astype(jnp.float32)
    dense_own = own_heads(w_dense, 0)
    fc1_own = lax.dynamic_slice_in_dim(w_fc1, mine * units, units, 1)
    fc1_bias = lax.dynamic_slice_in_dim(b_fc1, mine * units, units, 0).astype(jnp.float32)
    fc2_own = lax.dynamic_slice_in_dim(w_fc2, mine * units, units, 0)

    q_rows = 128
    padded = pl.cdiv(tree, q_rows) * q_rows
    tables = rotary_tables(padded, starts, parents)

    hidden_pre = dot32(normed, fc1_own, NN) + fc1_bias
    act_low = gelu_tanh(hidden_pre).astype(bf16)
    grad_fc2 = dot32(act_low, grad, TN).astype(bf16)
    sum_fc2 = lax.psum_scatter(grad_fc2, "rep", scatter_dimension=0, tiled=True)
    d_act = dot32(grad, fc2_own, NT)
    d_hidden_low = (d_act * gelu_slope(hidden_pre)).astype(bf16)

    def by_owner(partial):
        cols = partial.shape[1]
        return (
            partial.reshape(ctx, rep, row_split, cols)
            .transpose(1, 0, 2, 3)
            .reshape(model_width, cols)
        )

    def to_rows(summed):
        return lax.all_to_all(
            summed.reshape(ctx, row_split, summed.shape[1]), "ctx", 0, 0, tiled=True
        )

    grad_fc1 = dot32(normed, d_hidden_low, TN).astype(bf16)
    sum_fc1 = to_rows(
        lax.psum_scatter(by_owner(grad_fc1), "rep", scatter_dimension=0, tiled=True)
    )
    sum_fc1 = sum_fc1.transpose(1, 0, 2).reshape(row_split, ctx * units).astype(jnp.float32)

    qkv_pre = dot32(normed, qkv_own, NN) + qkv_bias
    d_attn_low = dot32(grad, dense_own, NT).astype(bf16)
    attn_low, d_qkv_low = tree_attention(
        starts, parents, qkv_pre, d_attn_low, tables, heads, width, q_rows
    )
    branches = lax.psum_scatter(
        (dot32(attn_low, dense_own, NN) + dot32(act_low, fc2_own, NN)).astype(bf16),
        ("ctx", "tp"),
        scatter_dimension=0,
        tiled=True,
    ).astype(jnp.float32)
    block_out = (
        (residual + branches + b_dense.astype(jnp.float32) + b_fc2.astype(jnp.float32))
        .astype(bf16)
        .reshape(tokens.shape)
    )
    grad_qkv = dot32(normed, d_qkv_low, TN).astype(bf16)
    if width > head_lanes:
        grad_qkv = grad_qkv.reshape(model_width, 3, width)[:, :, :head_lanes]
        grad_qkv = grad_qkv.reshape(model_width, 3 * head_lanes)
    sum_qkv = to_rows(
        lax.psum_scatter(by_owner(grad_qkv), "rep", scatter_dimension=0, tiled=True)
    )
    sum_qkv = (
        sum_qkv.reshape(ctx, row_split, 3, head_lanes)
        .transpose(1, 2, 0, 3)
        .reshape(row_split, 3, ctx * head_lanes)
        .astype(jnp.float32)
    )
    grad_dense = dot32(attn_low, grad, TN)[:head_lanes].astype(bf16)
    sum_dense = lax.psum_scatter(grad_dense, "rep", scatter_dimension=0, tiled=True)

    d_normed = lax.psum_scatter(
        (dot32(d_qkv_low, qkv_own, NT) + dot32(d_hidden_low, fc1_own, NT)).astype(bf16),
        ("ctx", "tp"),
        scatter_dimension=0,
        tiled=True,
    ).astype(jnp.float32)
    scaled = d_normed * gain_wide
    d_tokens = grad_own.astype(jnp.float32) + inv_std * (
        scaled
        - jnp.mean(scaled, axis=1, keepdims=True)
        - unit_norm * jnp.mean(scaled * unit_norm, axis=1, keepdims=True)
    )

    qkv_bias_grad = jnp.sum(d_qkv_low.astype(jnp.float32), axis=0).reshape(3, width)
    small = jnp.concatenate(
        [
            jnp.sum(d_hidden_low.astype(jnp.float32), axis=0).reshape(rep, units // rep),
            qkv_bias_grad[:, :head_lanes]
            .reshape(3, rep, head_lanes // rep)
            .transpose(1, 0, 2)
            .reshape(rep, 3 * head_lanes // rep),
            jnp.sum(
                lax.dynamic_slice_in_dim(grad, (lax.axis_index("tp") * ctx + mine) * head_lanes, head_lanes, 1)
                .astype(jnp.float32),
                axis=0,
            ).reshape(rep, head_lanes // rep),
        ],
        axis=1,
    )
    small = jnp.sum(lax.all_to_all(small, "rep", 0, 0, tiled=True), axis=0)
    fc1_bias_grad = small[: units // rep]
    qkv_bias_grad = small[units // rep : units // rep + 3 * head_lanes // rep].reshape(3, -1)
    out_bias_grad = small[units // rep + 3 * head_lanes // rep :]

    everyone = ("tp", "ctx", "rep")
    norm_grads = jnp.stack(
        [jnp.sum(d_normed * unit_norm, axis=0), jnp.sum(d_normed, axis=0)], axis=0
    )
    norm_grads = lax.psum(norm_grads, everyone)
    place = (lax.axis_index("tp") * ctx + mine) * rep + lax.axis_index("rep")
    share = model_width // (lax.axis_size("tp") * ctx * rep)
    norm_grads = lax.dynamic_slice_in_dim(norm_grads, place * share, share, 1)
    return (
        block_out,
        d_tokens.reshape(tokens.shape),
        norm_grads[0],
        norm_grads[1],
        sum_qkv,
        qkv_bias_grad,
        sum_dense.astype(jnp.float32),
        out_bias_grad,
        sum_fc1,
        fc1_bias_grad,
        sum_fc2.astype(jnp.float32),
        out_bias_grad,
    )


def solution(mesh):
    return jax.shard_map(
        shards,
        mesh=mesh,
        in_specs=(
            P("rep", "ctx", "tp", None),
            P("rep", "ctx", "tp", None),
            P("rep", "ctx"),
            P("rep", None),
            P("rep", None),
            P(),
            P(),
            P(None, None, "tp"),
            P(None, "tp"),
            P("tp", None),
            P(),
            P(None, "tp"),
            P("tp"),
            P("tp", None),
            P(),
        ),
        out_specs=(
            P("rep", "ctx", "tp", None),
            P("rep", "ctx", "tp", None),
            P(("tp", "ctx", "rep")),
            P(("tp", "ctx", "rep")),
            P(("ctx", "rep"), None, "tp"),
            P(None, ("tp", "ctx", "rep")),
            P(("tp", "ctx", "rep"), None),
            P(("tp", "ctx", "rep")),
            P(("ctx", "rep"), "tp"),
            P(("tp", "ctx", "rep")),
            P(("tp", "ctx", "rep"), None),
            P(("tp", "ctx", "rep")),
        ),
        check_vma=False,
    )
```

time: 1580 us -> 587 us (0.37)
  waiting for transfers between devices: 995 us -> 216 us
  matrix products: 260 us -> 104 us
  local copies, waits for them, and re-layouts: 140 us -> 31.5 us
  between operations: 15.6 us -> 84.4 us
  blocking collectives: 104 us -> 42.6 us
  Pallas kernels: 0 us -> 57.3 us
  other arithmetic: 47 us -> 28.4 us
    reduce_scatter x6, waiting for transfers between devices: 932 us -> 203 us  [the longest x1 75.4 us: shards(): sum_fc2 = lax.psum_scatter(grad_fc2, 'rep', scatter_dimension=0, tiled=True)]
    dot_general x44 -> x12, matrix products: 260 us -> 104 us  [dot32(): return lax.dot_general(lhs, rhs, dims, preferred_element_type=jnp.float32)]
    unnamed x2 -> x0, blocking collectives: 104 us -> none
    pallas_call x0 -> x1, Pallas kernels: none -> 57.3 us  [tree_attention(): pl.pallas_call(functools.partial(tree_attention_body, heads, width, token...]
    all_gather x4 -> x2, waiting for transfers between devices: 47.5 us -> 0.02 us  [the longest x1 0.02 us: shards(): grad = lax.all_gather(grad_own, ('ctx', 'tp'), axis=0, tiled=True)]
    psum x0 -> x1, blocking collectives: none -> 42.6 us  [shards(): norm_grads = lax.psum(norm_grads, everyone)]
    unnamed x74 -> x43, local copies, waits for them, and re-layouts: 47.7 us -> 8.02 us
    dynamic_update_slice x8 -> x0, local copies, waits for them, and re-layouts: 36.6 us -> none  [backward_one_block(): d_keyval = lax.dynamic_update_slice_in_dim(d_keyval, fresh, offset, 0)]
  transfers between devices with their start and end apart: 12 -> 11, of which waited for: 9 -> 6; matrix products, arithmetic and copies ran while one was open for 13% -> 24% of each run, Pallas kernels for 0% -> 0%
where the time goes in v1:
time: 587 us; the launch traced here: 578 us
  waiting for transfers between devices  216 us (37%)
  matrix products  104 us (18%)
  between operations  84.4 us (14%)
  Pallas kernels  57.3 us (10%)
  blocking collectives  42.6 us (7%)
  local copies, waits for them, and re-layouts  31.5 us (5%)
  other arithmetic  28.4 us (5%)
  starting transfers between devices  13.7 us (2%)
    dot_general x12, matrix products, dot32(): return lax.dot_general(lhs, rhs, dims, preferred_element_type=jnp.float32)  104 us
    reduce_scatter x1, waiting for transfers between devices, shards(): sum_fc2 = lax.psum_scatter(grad_fc2, 'rep', scatter_dimension=0, tiled=True)  75.4 us
    reduce_scatter x1, waiting for transfers between devices, shards(): lax.psum_scatter((dot32(attn_low, dense_own, NN) + dot32(act_low, fc2_own...  58.7 us
    pallas_call x1, Pallas kernels, tree_attention(): pl.pallas_call(functools.partial(tree_attention_body, heads, width, token...  57.3 us
    psum x1, blocking collectives, shards(): norm_grads = lax.psum(norm_grads, everyone)  42.6 us
    reduce_scatter x1, waiting for transfers between devices, shards(): lax.psum_scatter(by_owner(grad_fc1), 'rep', scatter_dimension=0, tiled=True)  34.9 us
    reduce_scatter x1, waiting for transfers between devices, shards(): lax.psum_scatter((dot32(d_qkv_low, qkv_own, NT) + dot32(d_hidden_low, fc1...  34.5 us
  transfers between devices with their start and end apart: 11, of which 6 were waited for; matrix products, arithmetic and copies ran while one was open for 24% of the time, Pallas kernels for 0%

profile of v1, /device:TPU:0, one launch (start us, length us, event | category | flops | bytes accessed | tf_op | source)
XLA Modules:
  0.0 577.9 jit_solution(12700931263672438723)
XLA Ops:
  12.7 2.5 fusion.45
  91.7 7.6 %select_convert_fusion = f32[1408]{0:T(1024)S(1)} fusion(s32[]{:T(128)S(6)} %add.478, s32[]{:T(128)} %bitcast.10, s32[]{:T(128)S(6)} %add.472, s32[]{:T(128)} %bitcast.40, s32[]{:T(128)S(6)} %add.466, s32[]{:T(128)} %bitcast.37, s32[]{:T(128)S(6)} %add.460, s32[]{:T(128)} %bitcast.34, s32[]{:T(128)S(6)} %add.454, s32[]{:T(128)} %bitcast.31, s32[]{:T(128)S(6)} %add.448, ...), kind=kLoop, calls=%fused_computation.81 | loop fusion | flops 68992 | bytes 5728 | tf_op jit(solution)/shard_map/convert_element_type | solution.py:52
  103.6 2.1 dynamic-slice_bitcast_fusion
  105.9 6.5 %fusion.32.grad_ref = bf16[1344,256]{1,0:T(8,128)(2,1)} fusion(bf16[1,1,1344,2048]{3,2,1,0:T(8,128)(2,1)} %all-gather.6.cloned.1.call-done, bf16[1024,2048]{1,0:T(8,128)(2,1)} %param.23, s32[]{:T(128)S(6)} %select_n.210), kind=kOutput, calls=%fused_computation.36 | convolution fusion | flops 1409630208 | bytes 7241732 | tf_op jit(solution)/shard_map/dot_general | solution.py:39
  112.4 9.1 %convolution_add_fusion.pre_ref = f32[1344,768]{1,0:T(8,128)} fusion(bf16[1344,2048]{1,0:T(8,128)(2,1)} %all-gather.4.cloned.1.call-done, f32[768]{0:T(1024)S(1)} %reshape.331, bf16[2048,256]{1,0:T(8,128)(2,1)S(1)} %get-tuple-element.45, bf16[2048,256]{1,0:T(8,128)(2,1)S(1)} %get-tuple-element.46, bf16[2048,256]{1,0:T(8,128)(2,1)S(1)} %get-tuple-element.44), kind=kOutput, calls=%fused_computation.22 | convolution fusion | flops 4238327808 | bytes 12782592 | tf_op jit(solution)/shard_map/dot_general | solution.py:39
  121.4 57.3 %tree_attention.1 = (bf16[1344,256]{1,0:T(8,128)(2,1)}, bf16[1344,768]{1,0:T(8,128)(2,1)}) custom-call(s32[13]{0:T(128)} %bitcast.172, s32[13]{0:T(128)} %bitcast.173, f32[1344,768]{1,0:T(8,128)} %convolution_add_fusion.pre_ref, bf16[1344,256]{1,0:T(8,128)(2,1)} %fusion.32.grad_ref, f32[1408,128]{1,0:T(8,128)} %copy.44.cos_ref, f32[1408,128]{1,0:T(8,128)} %copy.45.low_ref, ...), custom_call_target="tpu_custom_call" | custom-call | flops 13287555072 | bytes 8257536 | tf_op jit(solution)/shard_map/tree_attention/pallas_call | solution.py:286
  178.8 7.8 %convolution_convert_fusion.1 = bf16[2048,768]{1,0:T(8,128)(2,1)S(1)} fusion(bf16[1344,2048]{1,0:T(8,128)(2,1)} %all-gather.4.cloned.1.call-done, bf16[1344,768]{1,0:T(8,128)(2,1)} %get-tuple-element.15), kind=kOutput, calls=%fused_computation.31 | convolution fusion | flops 4229431296 | bytes 10715136 | tf_op jit(solution)/shard_map/dot_general | solution.py:39
  189.3 5.4 fusion.29
  194.8 10.1 %fusion.24 = f32[1344,1024]{1,0:T(8,128)S(1)} fusion(bf16[1344,2048]{1,0:T(8,128)(2,1)} %all-gather.4.cloned.1.call-done, bf16[2048,4096]{1,0:T(8,128)(2,1)} %param.25, s32[]{:T(128)S(6)} %select_n.259), kind=kOutput, calls=%fused_computation.29 | convolution fusion | flops 5637144576 | bytes 15204356 | tf_op jit(solution)/shard_map/dot_general | solution.py:39
  204.8 2.4 copy-done.18
  207.2 12.3 %convert_reduce_fusion = (f32[1024]{0:T(1024)S(1)}, bf16[1344,1024]{1,0:T(8,128)(2,1)S(1)}) fusion(f32[1344,1024]{1,0:T(8,128)S(1)} %fusion.24, f32[1024]{0:T(1024)S(1)} %dynamic-slice_convert_fusion, bf16[1,1,1344,2048]{3,2,1,0:T(8,128)(2,1)} %all-gather.6.cloned.1.call-done, bf16[4096,2048]{1,0:T(8,128)(2,1)} %param.27, s32[]{:T(128)S(6)} %select_n.259), kind=kOutput, calls=%fused_computation.19 | convolution fusion | flops 5667421184 | bytes 17965060 | tf_op jit(solution)/shard_map/dot_general | solution.py:39
  219.6 4.5 fusion.56
  224.1 10.1 %add_convert_fusion = bf16[1344,2048]{1,0:T(8,128)(2,1)} fusion(f32[1344,2048]{1,0:T(8,128)S(1)} %fusion.56, bf16[1344,1024]{1,0:T(8,128)(2,1)S(1)} %get-tuple-element.105, bf16[2048,4096]{1,0:T(8,128)(2,1)} %param.25, s32[]{:T(128)S(6)} %select_n.259), kind=kOutput, calls=%fused_computation | convolution fusion | flops 5642649600 | bytes 23461892 | tf_op jit(solution)/shard_map/dot_general | solution.py:39
  234.3 9.6 %convolution_convert_fusion = bf16[2048,1024]{1,0:T(8,128)(2,1)S(1)} fusion(bf16[1344,2048]{1,0:T(8,128)(2,1)} %all-gather.4.cloned.1.call-done, bf16[1344,1024]{1,0:T(8,128)(2,1)} %copy-done.19), kind=kOutput, calls=%fused_computation.24 | convolution fusion | flops 5639241728 | bytes 12451840 | tf_op jit(solution)/shard_map/dot_general | solution.py:39
  243.9 2.5 copy.51
  246.5 9.8 %fusion.21 = f32[1344,2048]{1,0:T(8,128)S(1)} fusion(bf16[4096,2048]{1,0:T(8,128)(2,1)} %param.27, s32[]{:T(128)S(6)} %select_n.259, f32[1344,1024]{1,0:T(8,128)} %copy-done.18, f32[1024]{0:T(1024)S(1)} %dynamic-slice_convert_fusion), kind=kOutput, calls=%fused_computation.26 | convolution fusion | flops 5650907136 | bytes 20713476 | tf_op jit(solution)/shard_map/dot_general | solution.py:39
  256.3 5.3 add_convert_fusion.1
  261.7 13.6 %fusion.17 = bf16[1024,2048]{1,0:T(8,128)(2,1)} fusion(bf16[1,1,1344,2048]{3,2,1,0:T(8,128)(2,1)} %all-gather.6.cloned.1.call-done, f32[1344,1024]{1,0:T(8,128)} %copy-done.18, f32[1024]{0:T(1024)S(1)} %dynamic-slice_convert_fusion), kind=kOutput, calls=%fused_computation.23 | convolution fusion | flops 5653004288 | bytes 15208448 | tf_op jit(solution)/shard_map/dot_general | solution.py:39
  277.9 6.3 %all-to-all-start.1 = ((f32[4,1,512]{2,1,0:T(1,128)}), f32[4,1,512]{2,1,0:T(1,128)S(1)}, u32[]{:S(2)}, u32[]{:S(2)}) async-start(f32[4,1,512]{2,1,0:T(1,128)} %all_to_all.13), calls=%async_computation.4 | async-start | bytes 16384 | tf_op jit(solution)/shard_map/all_to_all | solution.py:478
  284.2 2.3 copy.48
  286.5 3.3 all-to-all-done.1
  289.8 3.6 all-to-all-start
  296.5 8.4 %all-to-all-done = bf16[4,128,768]{1,2,0:T(8,128)(2,1)S(1)} async-done(((bf16[4,128,768]{1,2,0:T(8,128)(2,1)}), bf16[4,128,768]{1,2,0:T(8,128)(2,1)S(1)}, u32[]{:S(2)}, u32[]{:S(2)}) %all-to-all-start) | async-done | bytes 786464 | tf_op jit(solution)/shard_map/all_to_all | solution.py:407
  306.8 34.5 %reduce-scatter.9.cloned.1.call-done = bf16[168,2048]{1,0:T(8,128)(2,1)} async-done(((bf16[1344,2048]{1,0:T(8,128)(2,1)}), bf16[168,2048]{1,0:T(8,128)(2,1)}) %reduce-scatter.9.cloned.1.call-update) | async-done | bytes 688144 | tf_op jit(solution)/shard_map/reduce_scatter | solution.py:449
  343.2 42.6 %psum.7 = f32[2,2048]{1,0:T(2,128)S(1)} all-reduce(f32[2,2048]{1,0:T(2,128)S(1)} %pad_maximum_fusion.3), channel_id=1, replica_groups=mesh['tp'=2,'ctx'=4,'rep'=4] {'tp','ctx','rep'}, use_global_device_ids=true, to_apply=%region_8.9 | all-reduce | flops 4096 | bytes 32768 | tf_op jit(solution)/shard_map/psum | solution.py:487
  386.3 34.9 %reduce-scatter.15.cloned.1.call-done = bf16[512,1024]{1,0:T(8,128)(2,1)} async-done(((bf16[2048,1024]{1,0:T(8,128)(2,1)}), bf16[512,1024]{1,0:T(8,128)(2,1)}) %reduce-scatter.15.cloned.1.call-update) | async-done | bytes 1048592 | tf_op jit(solution)/shard_map/reduce_scatter | solution.py:413
  421.2 3.5 all-to-all-start.2
  424.8 58.7 %reduce-scatter.7.cloned.1.call-done = bf16[168,2048]{1,0:T(8,128)(2,1)} async-done(((bf16[1344,2048]{1,0:T(8,128)(2,1)}), bf16[168,2048]{1,0:T(8,128)(2,1)}) %reduce-scatter.7.cloned.1.call-update) | async-done | bytes 688144 | tf_op jit(solution)/shard_map/reduce_scatter | solution.py:422
  483.4 3.6 fusion.49
  487.1 75.4 %reduce-scatter.17.cloned.1.call-done = bf16[256,2048]{1,0:T(8,128)(2,1)} async-done(((bf16[1024,2048]{1,0:T(8,128)(2,1)}), bf16[256,2048]{1,0:T(8,128)(2,1)}) %reduce-scatter.17.cloned.1.call-update) | async-done | bytes 1048592 | tf_op jit(solution)/shard_map/reduce_scatter | solution.py:394
  562.5 2.8 convert_element_type.154
  567.4 2.9 copy.54
  (117 shorter events, 32.4 us)
Async XLA Ops:
  7.2 98.7 %all-gather.6.cloned.1.call-start = ((), (), s32[]{:S(2)}) async-start(), calls=%async_computation.16 | async-start | bytes 6193152 | tf_op jit(solution)/shard_map/all_gather | solution.py:369
  7.9 104.5 %all-gather.4.cloned.1.call-start = ((), (), s32[]{:S(2)}) async-start(), calls=%async_computation.9 | async-start | bytes 6193152 | tf_op jit(solution)/shard_map/all_gather | solution.py:368
  8.6 3.4 copy-start.9
  10.6 1.5 copy-start.11
  12.1 0.6 copy-start.13
  15.2 269.0 %reduce-scatter.11.cloned.1.call-start = ((), (), s32[]{:S(2)}) async-start(), calls=%async_computation.12 | async-start | bytes 3932160 | tf_op jit(solution)/shard_map/reduce_scatter | solution.py:438
  105.9 6.5 %copy-start.3 = (bf16[2048,256]{1,0:T(8,128)(2,1)}, bf16[2048,256]{1,0:T(8,128)(2,1)S(1)}, u32[]{:S(2)}) copy-start(bf16[2048,256]{1,0:T(8,128)(2,1)S(1)} %get-tuple-element.44) | copy-start | bytes 3145732
  105.9 6.5 %copy-start.5 = (bf16[2048,256]{1,0:T(8,128)(2,1)}, bf16[2048,256]{1,0:T(8,128)(2,1)S(1)}, u32[]{:S(2)}) copy-start(bf16[2048,256]{1,0:T(8,128)(2,1)S(1)} %get-tuple-element.45) | copy-start | bytes 3145732
  105.9 6.5 %copy-start.7 = (bf16[2048,256]{1,0:T(8,128)(2,1)}, bf16[2048,256]{1,0:T(8,128)(2,1)S(1)}, u32[]{:S(2)}) copy-start(bf16[2048,256]{1,0:T(8,128)(2,1)S(1)} %get-tuple-element.46) | copy-start | bytes 3145732
  186.6 2.7 copy-start.1
  188.6 106.1 %reduce-scatter.13.cloned.1.call-start = ((), (), s32[]{:S(2)}) async-start(), calls=%async_computation.13 | async-start | bytes 1310720 | tf_op jit(solution)/shard_map/reduce_scatter | solution.py:447
  194.7 146.6 %reduce-scatter.9.cloned.1.call-start = ((), (), s32[]{:S(2)}) async-start(), calls=%async_computation.11 | async-start | bytes 6193152 | tf_op jit(solution)/shard_map/reduce_scatter | solution.py:449
  204.8 2.4 copy-start.18
  207.2 12.3 %copy-start.2 = (bf16[1344,768]{1,0:T(8,128)(2,1)S(1)}, bf16[1344,768]{1,0:T(8,128)(2,1)}, u32[]{:S(2)}) copy-start(bf16[1344,768]{1,0:T(8,128)(2,1)} %get-tuple-element.15) | copy-start | bytes 6193156
  207.2 12.3 %copy-start.4 = (bf16[2048,256]{1,0:T(8,128)(2,1)S(1)}, bf16[2048,256]{1,0:T(8,128)(2,1)}, u32[]{:S(2)}) copy-start(bf16[2048,256]{1,0:T(8,128)(2,1)} %copy-done.3) | copy-start | bytes 3145732
  207.2 12.3 %copy-start.6 = (bf16[2048,256]{1,0:T(8,128)(2,1)S(1)}, bf16[2048,256]{1,0:T(8,128)(2,1)}, u32[]{:S(2)}) copy-start(bf16[2048,256]{1,0:T(8,128)(2,1)} %copy-done.5) | copy-start | bytes 3145732
  207.2 12.3 %copy-start.8 = (bf16[2048,256]{1,0:T(8,128)(2,1)S(1)}, bf16[2048,256]{1,0:T(8,128)(2,1)}, u32[]{:S(2)}) copy-start(bf16[2048,256]{1,0:T(8,128)(2,1)} %copy-done.7) | copy-start | bytes 3145732
  219.6 4.6 copy-start.19
  234.3 187.0 %reduce-scatter.15.cloned.1.call-start = ((), (), s32[]{:S(2)}) async-start(), calls=%async_computation.14 | async-start | bytes 5242880 | tf_op jit(solution)/shard_map/reduce_scatter | solution.py:413
  246.4 237.0 %reduce-scatter.7.cloned.1.call-start = ((), (), s32[]{:S(2)}) async-start(), calls=%async_computation.10 | async-start | bytes 6193152 | tf_op jit(solution)/shard_map/reduce_scatter | solution.py:422
  261.6 300.9 %reduce-scatter.17.cloned.1.call-start = ((), (), s32[]{:S(2)}) async-start(), calls=%async_computation.15 | async-start | bytes 5242880 | tf_op jit(solution)/shard_map/reduce_scatter | solution.py:394
  275.3 18.1 %copy-start.15 = (bf16[2048]{0:T(1024)(128)(2,1)S(1)}, bf16[2048]{0:T(1024)(128)(2,1)}, u32[]{:S(2)}) copy-start(bf16[2048]{0:T(1024)(128)(2,1)} %param.24) | copy-start | bytes 12292
  275.3 18.1 %copy-start.16 = (bf16[2048]{0:T(1024)(128)(2,1)S(1)}, bf16[2048]{0:T(1024)(128)(2,1)}, u32[]{:S(2)}) copy-start(bf16[2048]{0:T(1024)(128)(2,1)} %param.28) | copy-start | bytes 12292
  277.9 11.9 %all-to-all-start.1 = ((f32[4,1,512]{2,1,0:T(1,128)}), f32[4,1,512]{2,1,0:T(1,128)S(1)}, u32[]{:S(2)}, u32[]{:S(2)}) async-start(f32[4,1,512]{2,1,0:T(1,128)} %all_to_all.13), calls=%async_computation.4 | async-start | bytes 16384 | tf_op jit(solution)/shard_map/all_to_all | solution.py:478
  286.5 54.8 %copy-start = (bf16[1,1,168,2048]{3,2,1,0:T(8,128)(2,1)S(1)}, bf16[1,1,168,2048]{3,2,1,0:T(8,128)(2,1)}, u32[]{:S(2)}) copy-start(bf16[1,1,168,2048]{3,2,1,0:T(8,128)(2,1)} %param.15) | copy-start | bytes 2064388
  286.5 54.8 %copy-start.10 = (f32[2048]{0:T(1024)S(1)}, f32[2048]{0:T(1024)}, u32[]{:S(2)}) copy-start(f32[2048]{0:T(1024)} %copy-done.9) | copy-start | bytes 24580
  286.5 54.8 %copy-start.12 = (f32[168]{0:T(256)S(1)}, f32[168]{0:T(256)}, u32[]{:S(2)}) copy-start(f32[168]{0:T(256)} %copy-done.11) | copy-start | bytes 2020
  286.5 54.8 %copy-start.14 = (f32[168]{0:T(256)S(1)}, f32[168]{0:T(256)}, u32[]{:S(2)}) copy-start(f32[168]{0:T(256)} %copy-done.13) | copy-start | bytes 2020
  289.8 15.2 %all-to-all-start = ((bf16[4,128,768]{1,2,0:T(8,128)(2,1)}), bf16[4,128,768]{1,2,0:T(8,128)(2,1)S(1)}, u32[]{:S(2)}, u32[]{:S(2)}) async-start(bf16[4,128,768]{1,2,0:T(8,128)(2,1)} %copy.48), calls=%async_computation.3 | async-start | bytes 1572864 | tf_op jit(solution)/shard_map/all_to_all | solution.py:407
  293.5 276.8 %copy-start.17 = (f32[64]{0:T(128)}, f32[64]{0:T(128)S(1)}, u32[]{:S(2)}) copy-start(f32[64]{0:T(128)S(1)} %slice.182) | copy-start | bytes 772
  421.2 144.1 %all-to-all-start.2 = ((bf16[4,128,1024]{2,1,0:T(8,128)(2,1)}), bf16[4,128,1024]{2,1,0:T(8,128)(2,1)S(1)}, u32[]{:S(2)}, u32[]{:S(2)}) async-start(bf16[4,128,1024]{2,1,0:T(8,128)(2,1)} %bitcast.170), calls=%async_computation.7 | async-start | bytes 2097152 | tf_op jit(solution)/shard_map/all_to_all | solution.py:407
Sparse Core Ops, SparseCore 0:
  9.9 44.9 all-gather.5
  57.3 42.1 all-gather.3
  188.7 62.9 reduce-scatter.10
  253.8 27.1 reduce-scatter.12
  284.7 56.4 reduce-scatter.8
  343.4 77.7 reduce-scatter.14
  425.1 58.3 reduce-scatter.6
  485.7 76.7 reduce-scatter.16
